TPU v7x, 256 devices: a whole 4x4x8 slice. The times are simulated.
256 devices in a mesh: row: 8 (over x, core), col: 32 (over z, y).
Axes of the slice: x: 4, y: 4, z: 8, core: 2. Of those that a mesh axis runs over, the one named last changes fastest.
Arguments:
- matrix: float32 [24576, 12288], P('row', 'col'), may hold values from -6 to 6
Outputs:
- updated: float32 [24576, 12288], P('row', 'col')
All inputs are finite; a program needn't handle non-finite values.
Results may differ from a plain program's by a relative error of at most 0.0003.
Values sent between devices are 32-bit elements; how exact they have to be, the bound alone decides.
A program may use at most 64 MiB of HBM per device.

v0:
```python
import jax
import jax.numpy as jnp
from jax import lax
from jax.sharding import PartitionSpec as P

PANEL = 256
HIGHEST = lax.Precision.HIGHEST


def partner_2(block, axis, distance):
    count = lax.axis_size(axis)
    route = []
    for low in range(count):
        high = low | 1 << distance
        if high != low and high < count:
            route += [(low, high), (high, low)]
    return lax.ppermute(block, axis, route)


def broadcast(value, axis, source):
    kept = jnp.where(lax.axis_index(axis) == source, value, 0).astype(value.dtype)
    return lax.psum(kept, axis)


def upper_of(gram):
    return jnp.linalg.cholesky(gram).T


def combine_pair(upper_one, upper_two):
    gram = jnp.dot(upper_one.T, upper_one, precision=HIGHEST) + jnp.dot(
        upper_two.T, upper_two, precision=HIGHEST
    )
    return upper_of(gram)


def apply_inverse(upper, rows):
    return jax.scipy.linalg.solve_triangular(upper.T, rows.T, lower=True).T


def factor(panel):
    gram_local = lax.dot_general(panel, panel, (((0,), (0,)), ((), ())), precision=HIGHEST)
    is_first = lax.axis_index("row") == 0
    identity = jnp.eye(PANEL, dtype=jnp.float32)
    upper = upper_of(gram_local)
    for level in range(lax.axis_size("row").bit_length() - 1):
        partner = partner_2(upper, "row", level)
        upper = combine_pair(upper, partner)
    basis = apply_inverse(upper, panel)
    top_block = broadcast(basis[:PANEL], "row", 0)
    lead = identity + top_block
    vectors = basis.at[:PANEL].add(jnp.where(is_first, identity, jnp.zeros_like(identity)))
    return (vectors, lead)


def on_device(matrix):
    panel = matrix[:, :PANEL]
    vectors, lead = factor(panel)
    vectors, lead = (broadcast(vectors, "col", 0), broadcast(lead, "col", 0))
    partial_proj = lax.dot_general(vectors, matrix, (((0,), (0,)), ((), ())), precision=HIGHEST)
    projected = lax.psum(partial_proj, "row")
    lead_gram = jnp.dot(lead.T, lead, precision=HIGHEST)
    lead_factor = jnp.linalg.cholesky(lead_gram)
    coeffs = jax.scipy.linalg.cho_solve(
        (lead_factor, True), jnp.dot(lead.T, projected, precision=HIGHEST)
    )
    return matrix - jnp.dot(vectors, coeffs, precision=HIGHEST)


def solution(mesh):
    in_specs = (P("row", "col"),)
    out_specs = P("row", "col")
    return jax.shard_map(
        on_device, mesh=mesh, in_specs=in_specs, out_specs=out_specs, check_vma=False
    )
```

profile of v0, /device:TPU:8, one launch (start us, length us, event | category | flops | bytes accessed | tf_op | source)
XLA Modules:
  0.0 583.5 jit_solution(9986484635231155321)
XLA Ops:
  6.5 7.9 %fusion.1 = f32[256,256]{1,0:T(8,128)S(1)} fusion(f32[3072,384]{1,0:T(8,128)} %param.4), kind=kOutput, calls=%fused_computation.11 | convolution fusion | flops 2415919104 | bytes 3407872 | tf_op jit(solution)/shard_map/dot_general | solution.py:41
  14.7 11.7 %cholesky.256 = f32[128,128]{1,0:T(8,128)S(1)} custom-call(f32[128,128]{1,0:T(8,128)S(1)} %cholesky.422), custom_call_target="Cholesky" | custom-call | tf_op jit(solution)/shard_map/jit(cholesky)/cholesky | solution.py:26
  26.4 9.8 %custom-call.25 = f32[1,128,128]{1,2,0:T(8,128)S(1)} custom-call(f32[1,128,128]{2,1,0:T(8,128)S(1)} %get-tuple-element.77), custom_call_target="InvertDiagBlocksLowerTriangular" | custom-call | tf_op jit(solution)/shard_map/jit(cholesky)/cholesky | solution.py:26
  36.8 11.9 %cholesky.273 = f32[128,128]{1,0:T(8,128)S(1)} custom-call(f32[128,128]{1,0:T(8,128)S(1)} %convolution_subtract_fusion.5), custom_call_target="Cholesky" | custom-call | tf_op jit(solution)/shard_map/jit(cholesky)/cholesky | solution.py:26
  53.0 11.7 %cholesky.290 = f32[128,128]{1,0:T(8,128)S(1)} custom-call(f32[128,128]{1,0:T(8,128)S(1)} %cholesky.425), custom_call_target="Cholesky" | custom-call | tf_op jit(solution)/shard_map/jit(cholesky)/cholesky | solution.py:26
  64.8 9.8 %custom-call.26 = f32[1,128,128]{1,2,0:T(8,128)S(1)} custom-call(f32[1,128,128]{2,1,0:T(8,128)S(1)} %get-tuple-element.73), custom_call_target="InvertDiagBlocksLowerTriangular" | custom-call | tf_op jit(solution)/shard_map/jit(cholesky)/cholesky | solution.py:26
  75.1 11.7 %cholesky.307 = f32[128,128]{1,0:T(8,128)S(1)} custom-call(f32[128,128]{1,0:T(8,128)S(1)} %slice_subtract_fusion.2), custom_call_target="Cholesky" | custom-call | tf_op jit(solution)/shard_map/jit(cholesky)/cholesky | solution.py:26
  99.0 11.7 %cholesky.324 = f32[128,128]{1,0:T(8,128)S(1)} custom-call(f32[128,128]{1,0:T(8,128)S(1)} %cholesky.428), custom_call_target="Cholesky" | custom-call | tf_op jit(solution)/shard_map/jit(cholesky)/cholesky | solution.py:26
  110.8 9.8 %custom-call.27 = f32[1,128,128]{1,2,0:T(8,128)S(1)} custom-call(f32[1,128,128]{2,1,0:T(8,128)S(1)} %get-tuple-element.69), custom_call_target="InvertDiagBlocksLowerTriangular" | custom-call | tf_op jit(solution)/shard_map/jit(cholesky)/cholesky | solution.py:26
  121.1 11.7 %cholesky.341 = f32[128,128]{1,0:T(8,128)S(1)} custom-call(f32[128,128]{1,0:T(8,128)S(1)} %slice_subtract_fusion.1), custom_call_target="Cholesky" | custom-call | tf_op jit(solution)/shard_map/jit(cholesky)/cholesky | solution.py:26
  145.3 11.7 %cholesky.358 = f32[128,128]{1,0:T(8,128)S(1)} custom-call(f32[128,128]{1,0:T(8,128)S(1)} %cholesky.431), custom_call_target="Cholesky" | custom-call | tf_op jit(solution)/shard_map/jit(cholesky)/cholesky | solution.py:26
  157.1 9.8 %custom-call.28 = f32[1,128,128]{1,2,0:T(8,128)S(1)} custom-call(f32[1,128,128]{2,1,0:T(8,128)S(1)} %get-tuple-element.65), custom_call_target="InvertDiagBlocksLowerTriangular" | custom-call | tf_op jit(solution)/shard_map/jit(cholesky)/cholesky | solution.py:26
  167.4 11.7 %cholesky.375 = f32[128,128]{1,0:T(8,128)S(1)} custom-call(f32[128,128]{1,0:T(8,128)S(1)} %slice_subtract_fusion), custom_call_target="Cholesky" | custom-call | tf_op jit(solution)/shard_map/jit(cholesky)/cholesky | solution.py:26
  185.8 19.7 %custom-call.19 = f32[2,128,128]{1,2,0:T(8,128)S(1)} custom-call(f32[2,128,128]{2,1,0:T(8,128)S(1)} %get-tuple-element.25), custom_call_target="InvertDiagBlocksLowerTriangular" | custom-call | tf_op jit(solution)/shard_map/jit(_solve_triangular)/triangular_solve | solution.py:37
  221.5 66.5 %all-reduce.6.cloned.1.call-done = f32[256,256]{1,0:T(8,128)} async-done(((f32[256,256]{1,0:T(8,128)}), f32[256,256]{1,0:T(8,128)}) %all-reduce.6.cloned.1.call-update) | async-done | bytes 262160 | tf_op jit(solution)/shard_map/psum | solution.py:22
  290.1 159.1 %all-reduce.10.cloned.1.call-done = (f32[3072,256]{1,0:T(8,128)}, f32[256,256]{1,0:T(8,128)}) async-done(((f32[3072,256]{1,0:T(8,128)}, f32[256,256]{1,0:T(8,128)}), (f32[3072,256]{1,0:T(8,128)}, f32[256,256]{1,0:T(8,128)})) %all-reduce.10.cloned.1.call-update) | async-done | bytes 3407888 | tf_op jit(solution)/shard_map/psum | solution.py:22
  453.6 11.7 %cholesky.392 = f32[128,128]{1,0:T(8,128)S(1)} custom-call(f32[128,128]{1,0:T(8,128)S(1)} %cholesky.434), custom_call_target="Cholesky" | custom-call | tf_op jit(solution)/shard_map/jit(cholesky)/cholesky | solution.py:62
  465.3 9.8 %custom-call.29 = f32[1,128,128]{1,2,0:T(8,128)S(1)} custom-call(f32[1,128,128]{2,1,0:T(8,128)S(1)} %get-tuple-element.61), custom_call_target="InvertDiagBlocksLowerTriangular" | custom-call | tf_op jit(solution)/shard_map/jit(cholesky)/cholesky | solution.py:62
  477.3 11.7 %cholesky.409 = f32[128,128]{1,0:T(8,128)S(1)} custom-call(f32[128,128]{1,0:T(8,128)S(1)} %convolution_subtract_fusion.4), custom_call_target="Cholesky" | custom-call | tf_op jit(solution)/shard_map/jit(cholesky)/cholesky | solution.py:62
  490.5 8.0 %fusion.79 = f32[256,384]{1,0:T(8,128)} fusion(f32[3072,256]{1,0:T(8,128)S(1)} %copy-done.1, f32[3072,384]{1,0:T(8,128)} %param.4), kind=kOutput, calls=%fused_computation.151 | convolution fusion | flops 3623878656 | bytes 8257536 | tf_op jit(solution)/shard_map/dot_general | solution.py:59
  501.5 5.7 while.4
  507.8 20.5 %custom-call.20 = f32[2,128,128]{1,2,0:T(8,128)S(1)} custom-call(f32[2,128,128]{2,1,0:T(8,128)} %copy-done.5), custom_call_target="InvertDiagBlocksLowerTriangular" | custom-call | tf_op jit(solution)/shard_map/jit(_cho_solve)/triangular_solve | solution.py:63
  528.3 34.7 %all-reduce.8.cloned.1.call-done = f32[256,384]{1,0:T(8,128)} async-done(((f32[256,384]{1,0:T(8,128)}), f32[256,384]{1,0:T(8,128)}) %all-reduce.8.cloned.1.call-update) | async-done | bytes 393232 | tf_op jit(solution)/shard_map/psum | solution.py:60
  568.4 8.4 %convolution_subtract_fusion = f32[3072,384]{1,0:T(8,128)} fusion(f32[3072,384]{1,0:T(8,128)} %param.4, f32[3072,256]{1,0:T(8,128)S(1)} %copy-done.1, f32[128,384]{1,0:T(8,128)S(1)} %fusion.65, f32[128,384]{1,0:T(8,128)S(1)} %fusion.64), kind=kOutput, calls=%fused_computation.4 | convolution fusion | flops 3625156608 | bytes 12976128 | tf_op jit(solution)/shard_map/dot_general | solution.py:66
  (118 shorter events, 75.9 us)
Async XLA Ops:
  6.5 281.4 %all-reduce.6.cloned.1.call-start = ((), (), s32[]{:S(2)}) async-start(), calls=%async_computation | async-start | bytes 524288 | tf_op jit(solution)/shard_map/psum | solution.py:22
  50.8 1.6 collective-permute-start
  89.6 8.8 %collective-permute-start.1 = (f32[256,256]{0,1:T(8,128)S(1)}, f32[256,256]{0,1:T(8,128)S(1)}, u32[]{:S(2)}, u32[]{:S(2)}) collective-permute-start(f32[256,256]{0,1:T(8,128)S(1)} %fusion.20), channel_id=1, source_target_pairs={{0,64},{64,0},{32,96},{96,32},{128,192},{192,128},{160,224},{224,1... | collective-permute-start | bytes 786440 | tf_op jit(solution)/shard_map/ppermute | solution.py:17
  135.5 9.3 %collective-permute-start.2 = (f32[256,256]{0,1:T(8,128)S(1)}, f32[256,256]{0,1:T(8,128)S(1)}, u32[]{:S(2)}, u32[]{:S(2)}) collective-permute-start(f32[256,256]{0,1:T(8,128)S(1)} %fusion.22), channel_id=1, source_target_pairs={{0,128},{128,0},{32,160},{160,32},{64,192},{192,64},{96,224},{224,... | collective-permute-start | bytes 786440 | tf_op jit(solution)/shard_map/ppermute | solution.py:17
  217.9 1.7 copy-start
  219.5 229.7 %all-reduce.10.cloned.1.call-start = ((), (), s32[]{:S(2)}) async-start(), calls=%async_computation.2 | async-start | bytes 6815744 | tf_op jit(solution)/shard_map/psum | solution.py:22
  289.7 273.3 %all-reduce.8.cloned.1.call-start = ((), (), s32[]{:S(2)}) async-start(), calls=%async_computation.1 | async-start | bytes 786432 | tf_op jit(solution)/shard_map/psum | solution.py:60
  449.2 41.2 %copy-start.1 = (f32[3072,256]{1,0:T(8,128)S(1)}, f32[3072,256]{1,0:T(8,128)}, u32[]{:S(2)}) copy-start(f32[3072,256]{1,0:T(8,128)} %get-tuple-element.50) | copy-start | bytes 9437188
  452.8 0.7 copy-start.4
  489.1 1.4 copy-start.3
  490.5 72.5 %copy-start.2 = (f32[256,256]{1,0:T(8,128)S(1)}, f32[256,256]{1,0:T(8,128)}, u32[]{:S(2)}) copy-start(f32[256,256]{1,0:T(8,128)} %get-tuple-element.51) | copy-start | bytes 786436
  507.2 0.6 copy-start.5
Sparse Core Ops, SparseCore 0:
  219.7 68.2 all-reduce.5
  291.6 157.5 all-reduce.9
  498.6 64.3 all-reduce.7
where the time goes:
time: 593 us; the launch traced here: 583 us
  waiting for transfers between devices  270 us (46%)
  other arithmetic  220 us (37%)
  matrix products  48.8 us (8%)
  between operations  20.2 us (3%)
  local copies, waits for them, and re-layouts  18.1 us (3%)
    psum x2, waiting for transfers between devices, broadcast(): return lax.psum(kept, axis)  226 us
    another operation x27, other arithmetic, upper_of(): return jnp.linalg.cholesky(gram).T  138 us
    another operation x7, other arithmetic, on_device(): lead_factor = jnp.linalg.cholesky(lead_gram)  34.7 us
    psum x1, waiting for transfers between devices, on_device(): projected = lax.psum(partial_proj, 'row')  34.7 us
    another operation x2, other arithmetic, on_device(): jax.scipy.linalg.cho_solve((lead_factor, True), jnp.dot(lead.T, projected...  22.2 us
    another operation x3, other arithmetic, apply_inverse(): return jax.scipy.linalg.solve_triangular(upper.T, rows.T, lower=True).T  19.7 us
  transfers between devices with their start and end apart: 6, of which 6 were waited for; matrix products, arithmetic and copies ran while one was open for 6% of the time, Pallas kernels for 0%

commit v1 on v0

--- a/solution.py
+++ b/solution.py
@@ -57,7 +57,7 @@
     vectors, lead = factor(panel)
     vectors, lead = (broadcast(vectors, "col", 0), broadcast(lead, "col", 0))
     partial_proj = lax.dot_general(vectors, matrix, (((0,), (0,)), ((), ())), precision=HIGHEST)
-    projected = lax.psum(partial_proj, "row")
+    projected = jnp.sum(jax.lax.all_gather(partial_proj, "row"), 0)
     lead_gram = jnp.dot(lead.T, lead, precision=HIGHEST)
     lead_factor = jnp.linalg.cholesky(lead_gram)
     coeffs = jax.scipy.linalg.cho_solve(

time: 593 us -> 554 us (0.934)
  waiting for transfers between devices: 270 us -> 235 us
    psum x1 -> x0, waiting for transfers between devices: 34.7 us -> none  [on_device(): projected = lax.psum(partial_proj, 'row')]
  transfers between devices with their start and end apart: 6 -> 6, of which waited for: 6 -> 5; matrix products, arithmetic and copies ran while one was open for 6% -> 12% of each run, Pallas kernels for 0% -> 0%
where the time goes in v1:
time: 554 us; the launch traced here: 543 us
  waiting for transfers between devices  235 us (42%)
  other arithmetic  220 us (40%)
  matrix products  47.2 us (9%)
  between operations  20.2 us (4%)
  local copies, waits for them, and re-layouts  14.3 us (3%)
  starting transfers between devices  5.84 us (1%)
    psum x2, waiting for transfers between devices, broadcast(): return lax.psum(kept, axis)  226 us
    another operation x27, other arithmetic, upper_of(): return jnp.linalg.cholesky(gram).T  138 us
    another operation x7, other arithmetic, on_device(): lead_factor = jnp.linalg.cholesky(lead_gram)  34.7 us
    another operation x3, other arithmetic, apply_inverse(): return jax.scipy.linalg.solve_triangular(upper.T, rows.T, lower=True).T  19.7 us
    another operation x2, other arithmetic, on_device(): jax.scipy.linalg.cho_solve((lead_factor, True), jnp.dot(lead.T, projected...  19.7 us
  transfers between devices with their start and end apart: 6, of which 5 were waited for; matrix products, arithmetic and copies ran while one was open for 12% of the time, Pallas kernels for 0%

profile of v1, /device:TPU:8, one launch (start us, length us, event | category | flops | bytes accessed | tf_op | source)
XLA Modules:
  0.0 542.9 jit_solution(13848568304484892200)
XLA Ops:
  6.5 7.9 %fusion.1 = f32[256,256]{1,0:T(8,128)S(1)} fusion(f32[3072,384]{1,0:T(8,128)} %param.4), kind=kOutput, calls=%fused_computation.11 | convolution fusion | flops 2415919104 | bytes 3407872 | tf_op jit(solution)/shard_map/dot_general | solution.py:41
  14.7 11.7 %cholesky.256 = f32[128,128]{1,0:T(8,128)S(1)} custom-call(f32[128,128]{1,0:T(8,128)S(1)} %cholesky.422), custom_call_target="Cholesky" | custom-call | tf_op jit(solution)/shard_map/jit(cholesky)/cholesky | solution.py:26
  26.4 9.8 %custom-call.25 = f32[1,128,128]{1,2,0:T(8,128)S(1)} custom-call(f32[1,128,128]{2,1,0:T(8,128)S(1)} %get-tuple-element.77), custom_call_target="InvertDiagBlocksLowerTriangular" | custom-call | tf_op jit(solution)/shard_map/jit(cholesky)/cholesky | solution.py:26
  36.8 11.9 %cholesky.273 = f32[128,128]{1,0:T(8,128)S(1)} custom-call(f32[128,128]{1,0:T(8,128)S(1)} %convolution_subtract_fusion.5), custom_call_target="Cholesky" | custom-call | tf_op jit(solution)/shard_map/jit(cholesky)/cholesky | solution.py:26
  53.0 11.7 %cholesky.290 = f32[128,128]{1,0:T(8,128)S(1)} custom-call(f32[128,128]{1,0:T(8,128)S(1)} %cholesky.425), custom_call_target="Cholesky" | custom-call | tf_op jit(solution)/shard_map/jit(cholesky)/cholesky | solution.py:26
  64.8 9.8 %custom-call.26 = f32[1,128,128]{1,2,0:T(8,128)S(1)} custom-call(f32[1,128,128]{2,1,0:T(8,128)S(1)} %get-tuple-element.73), custom_call_target="InvertDiagBlocksLowerTriangular" | custom-call | tf_op jit(solution)/shard_map/jit(cholesky)/cholesky | solution.py:26
  75.1 11.7 %cholesky.307 = f32[128,128]{1,0:T(8,128)S(1)} custom-call(f32[128,128]{1,0:T(8,128)S(1)} %slice_subtract_fusion.2), custom_call_target="Cholesky" | custom-call | tf_op jit(solution)/shard_map/jit(cholesky)/cholesky | solution.py:26
  99.0 11.7 %cholesky.324 = f32[128,128]{1,0:T(8,128)S(1)} custom-call(f32[128,128]{1,0:T(8,128)S(1)} %cholesky.428), custom_call_target="Cholesky" | custom-call | tf_op jit(solution)/shard_map/jit(cholesky)/cholesky | solution.py:26
  110.8 9.8 %custom-call.27 = f32[1,128,128]{1,2,0:T(8,128)S(1)} custom-call(f32[1,128,128]{2,1,0:T(8,128)S(1)} %get-tuple-element.69), custom_call_target="InvertDiagBlocksLowerTriangular" | custom-call | tf_op jit(solution)/shard_map/jit(cholesky)/cholesky | solution.py:26
  121.1 11.7 %cholesky.341 = f32[128,128]{1,0:T(8,128)S(1)} custom-call(f32[128,128]{1,0:T(8,128)S(1)} %slice_subtract_fusion.1), custom_call_target="Cholesky" | custom-call | tf_op jit(solution)/shard_map/jit(cholesky)/cholesky | solution.py:26
  139.2 5.6 %collective-permute-done.2 = f32[256,256]{0,1:T(8,128)S(1)} collective-permute-done((f32[256,256]{0,1:T(8,128)S(1)}, f32[256,256]{0,1:T(8,128)S(1)}, u32[]{:S(2)}, u32[]{:S(2)}) %collective-permute-start.2) | collective-permute-done | bytes 262176 | tf_op jit(solution)/shard_map/ppermute | solution.py:17
  145.3 11.7 %cholesky.358 = f32[128,128]{1,0:T(8,128)S(1)} custom-call(f32[128,128]{1,0:T(8,128)S(1)} %cholesky.431), custom_call_target="Cholesky" | custom-call | tf_op jit(solution)/shard_map/jit(cholesky)/cholesky | solution.py:26
  157.1 9.8 %custom-call.28 = f32[1,128,128]{1,2,0:T(8,128)S(1)} custom-call(f32[1,128,128]{2,1,0:T(8,128)S(1)} %get-tuple-element.65), custom_call_target="InvertDiagBlocksLowerTriangular" | custom-call | tf_op jit(solution)/shard_map/jit(cholesky)/cholesky | solution.py:26
  167.4 11.7 %cholesky.375 = f32[128,128]{1,0:T(8,128)S(1)} custom-call(f32[128,128]{1,0:T(8,128)S(1)} %slice_subtract_fusion), custom_call_target="Cholesky" | custom-call | tf_op jit(solution)/shard_map/jit(cholesky)/cholesky | solution.py:26
  185.8 19.7 %custom-call.19 = f32[2,128,128]{1,2,0:T(8,128)S(1)} custom-call(f32[2,128,128]{2,1,0:T(8,128)S(1)} %get-tuple-element.25), custom_call_target="InvertDiagBlocksLowerTriangular" | custom-call | tf_op jit(solution)/shard_map/jit(_solve_triangular)/triangular_solve | solution.py:37
  208.4 5.2 convolution_subtract_fusion.1
  221.5 66.5 %all-reduce.5.cloned.1.call-done = f32[256,256]{1,0:T(8,128)} async-done(((f32[256,256]{1,0:T(8,128)}), f32[256,256]{1,0:T(8,128)}) %all-reduce.5.cloned.1.call-update) | async-done | bytes 262160 | tf_op jit(solution)/shard_map/psum | solution.py:22
  290.1 159.1 %all-reduce.7.cloned.1.call-done = (f32[3072,256]{1,0:T(8,128)}, f32[256,256]{1,0:T(8,128)}) async-done(((f32[3072,256]{1,0:T(8,128)}, f32[256,256]{1,0:T(8,128)}), (f32[3072,256]{1,0:T(8,128)}, f32[256,256]{1,0:T(8,128)})) %all-reduce.7.cloned.1.call-update) | async-done | bytes 3407888 | tf_op jit(solution)/shard_map/psum | solution.py:22
  449.2 9.2 %fusion.79 = f32[256,384]{1,0:T(8,128)} fusion(f32[3072,256]{1,0:T(8,128)} %get-tuple-element.50, f32[3072,384]{1,0:T(8,128)} %param.4), kind=kOutput, calls=%fused_computation.151 | convolution fusion | flops 3623878656 | bytes 8257536 | tf_op jit(solution)/shard_map/dot_general | solution.py:59
  459.3 11.7 %cholesky.392 = f32[128,128]{1,0:T(8,128)S(1)} custom-call(f32[128,128]{1,0:T(8,128)S(1)} %cholesky.434), custom_call_target="Cholesky" | custom-call | tf_op jit(solution)/shard_map/jit(cholesky)/cholesky | solution.py:62
  471.1 9.9 %custom-call.29 = f32[1,128,128]{1,2,0:T(8,128)S(1)} custom-call(f32[1,128,128]{2,1,0:T(8,128)S(1)} %get-tuple-element.61), custom_call_target="InvertDiagBlocksLowerTriangular" | custom-call | tf_op jit(solution)/shard_map/jit(cholesky)/cholesky | solution.py:62
  481.5 11.7 %cholesky.409 = f32[128,128]{1,0:T(8,128)S(1)} custom-call(f32[128,128]{1,0:T(8,128)S(1)} %convolution_subtract_fusion.4), custom_call_target="Cholesky" | custom-call | tf_op jit(solution)/shard_map/jit(cholesky)/cholesky | solution.py:62
  499.7 19.7 %custom-call.20 = f32[2,128,128]{1,2,0:T(8,128)S(1)} custom-call(f32[2,128,128]{2,1,0:T(8,128)S(1)} %get-tuple-element.33), custom_call_target="InvertDiagBlocksLowerTriangular" | custom-call | tf_op jit(solution)/shard_map/jit(_cho_solve)/triangular_solve | solution.py:63
  527.8 8.4 %convolution_subtract_fusion = f32[3072,384]{1,0:T(8,128)} fusion(f32[3072,384]{1,0:T(8,128)} %param.4, f32[3072,256]{1,0:T(8,128)S(1)} %copy-done.1, f32[128,384]{1,0:T(8,128)S(1)} %fusion.65, f32[128,384]{1,0:T(8,128)S(1)} %fusion.64), kind=kOutput, calls=%fused_computation.4 | convolution fusion | flops 3625156608 | bytes 12976128 | tf_op jit(solution)/shard_map/dot_general | solution.py:66
  (115 shorter events, 62.5 us)
Async XLA Ops:
  6.5 281.4 %all-reduce.5.cloned.1.call-start = ((), (), s32[]{:S(2)}) async-start(), calls=%async_computation | async-start | bytes 524288 | tf_op jit(solution)/shard_map/psum | solution.py:22
  50.8 1.6 collective-permute-start
  89.6 8.8 %collective-permute-start.1 = (f32[256,256]{0,1:T(8,128)S(1)}, f32[256,256]{0,1:T(8,128)S(1)}, u32[]{:S(2)}, u32[]{:S(2)}) collective-permute-start(f32[256,256]{0,1:T(8,128)S(1)} %fusion.20), channel_id=1, source_target_pairs={{0,64},{64,0},{32,96},{96,32},{128,192},{192,128},{160,224},{224,1... | collective-permute-start | bytes 786440 | tf_op jit(solution)/shard_map/ppermute | solution.py:17
  135.5 9.3 %collective-permute-start.2 = (f32[256,256]{0,1:T(8,128)S(1)}, f32[256,256]{0,1:T(8,128)S(1)}, u32[]{:S(2)}, u32[]{:S(2)}) collective-permute-start(f32[256,256]{0,1:T(8,128)S(1)} %fusion.22), channel_id=1, source_target_pairs={{0,128},{128,0},{32,160},{160,32},{64,192},{192,64},{96,224},{224,... | collective-permute-start | bytes 786440 | tf_op jit(solution)/shard_map/ppermute | solution.py:17
  217.9 1.7 copy-start
  219.5 229.7 %all-reduce.7.cloned.1.call-start = ((), (), s32[]{:S(2)}) async-start(), calls=%async_computation.2 | async-start | bytes 6815744 | tf_op jit(solution)/shard_map/psum | solution.py:22
  289.7 229.7 %all-gather.3.cloned.1.call-start = ((), (), s32[]{:S(2)}) async-start(), calls=%async_computation.1 | async-start | bytes 3538944 | tf_op jit(solution)/shard_map/all_gather | solution.py:60
  449.2 9.3 %copy-start.2 = (f32[256,256]{1,0:T(8,128)S(1)}, f32[256,256]{1,0:T(8,128)}, u32[]{:S(2)}) copy-start(f32[256,256]{1,0:T(8,128)} %get-tuple-element.51) | copy-start | bytes 786436
  499.7 19.7 %copy-start.3 = (f32[256,256]{1,0:T(8,128)}, f32[256,256]{1,0:T(8,128)S(1)}, u32[]{:S(2)}) copy-start(f32[256,256]{1,0:T(8,128)S(1)} %get-tuple-element.190) | copy-start | bytes 786436
  519.4 8.4 %copy-start.1 = (f32[3072,256]{1,0:T(8,128)S(1)}, f32[3072,256]{1,0:T(8,128)}, u32[]{:S(2)}) copy-start(f32[3072,256]{1,0:T(8,128)} %get-tuple-element.50) | copy-start | bytes 9437188
Sparse Core Ops, SparseCore 0:
  219.7 68.2 all-reduce.4
  291.6 157.5 all-reduce.6
  458.6 28.7 all-gather.2
